TPU v7x, 512 devices: a whole 4x4x16 slice. The times are simulated.
512 devices in a mesh: seq: 16 (over y, x), table: 32 (over z, core).
Axes of the slice: x: 4, y: 4, z: 16, core: 2. Of those that a mesh axis runs over, the one named last changes fastest.
Arguments:
- events_x: bfloat16 [32, 2048, 512], P('table', 'seq'), may hold values from -6 to 6
- proj: bfloat16 [512, 1536], replicated, may hold values from -0.25 to 0.25
- out_grad: bfloat16 [32, 2048, 512], P('table', 'seq'), may hold values from -6 to 6
- block_mask: int32 [16, 16], replicated, may hold values 0 or 1
- item_ids: int32 [32, 2048], P('table', 'seq'), may hold values from 0 to 16383, as said below
- owner_of: int32 [16384], replicated, may hold values from 0 to 31, as said below
- local_of: int32 [16384], replicated, may hold values from 0 to 511, as said below
- table: bfloat16 [16384, 512], P('table'), may hold values from -3 to 3
- moment: float32 [16384, 512], P('table'), may hold values from -2 to 2
- second: float32 [16384], P('table'), may hold values from 0.05 to 2
Outputs:
- new_table: bfloat16 [16384, 512], P('table')
- new_moment: float32 [16384, 512], P('table')
- new_second: float32 [16384], P('table')
- event_rows: bfloat16 [32, 2048, 512], P('table', 'seq')
Inputs may be any that keep to these rules, and one draw needn't show every extreme that they name: `item_ids`: among the 128 events of one device (one history, one seq index), at most 8 have items of one owner (owner_of); in every draw, for each seq index, some owner gets exactly 8 from the device of every history. owner_of[r] * 512 + local_of[r] takes every value of 0 to 16383 once over the items r. `local_of`: see owner_of.
All inputs are finite; a program needn't handle non-finite values.
Results may differ from a plain program's by a relative error of at most 0.0075.
Values may be sent and summed in bfloat16 or wider, within the bound.
No kernel may reach another device: no remote copies, remote signals or barrier semaphores. Data moves between devices by JAX's collectives and lax.ppermute only.
A program may use at most 64 MiB of HBM per device.

v0:
```python
import math
import jax
import jax.numpy as jnp
from jax import lax
from jax.sharding import PartitionSpec as P

HEADS = 8
first_decay = 0.9
second_decay = 0.99
step_rate = 0.05
epsilon = 1e-08


def block_length(piece_rows):
    block_rows = piece_rows
    while block_rows > 1024 and block_rows % 2 == 0:
        block_rows = block_rows // 2
    return block_rows


def adam_update(item_grad, moment, second, table):
    new_moment = first_decay * moment + (1.0 - first_decay) * item_grad
    new_second = second_decay * second + (1.0 - second_decay) * jnp.mean(
        item_grad * item_grad, axis=1
    )
    new_table = (
        table.astype(jnp.float32)
        - step_rate * new_moment / (jnp.sqrt(new_second) + epsilon)[:, None]
    ).astype(jnp.bfloat16)
    return (new_table, new_moment, new_second)


def body(events_x, proj, out_grad, block_mask, item_ids, owner_of, local_of, table, moment, second):
    tokens = events_x.shape[1]
    features = events_x.shape[2]
    head_size = features // HEADS
    seq_count = lax.axis_size("seq")
    owner_count = lax.axis_size("table")
    position = lax.axis_index("seq")
    history_scale = 1.0 / math.sqrt(tokens * seq_count)
    temper = 1.0 / math.sqrt(head_size)
    block_ids = jnp.arange(seq_count)
    inputs = events_x[0]
    cotangent = out_grad[0]
    projected = jnp.dot(inputs, proj, preferred_element_type=jnp.float32).astype(jnp.bfloat16)
    queries = projected[:, :features]
    key_mat = projected[:, features : 2 * features]
    value_mat = projected[:, 2 * features :]
    own_pos = position * tokens + jnp.arange(tokens)
    visible_col = lax.dynamic_slice_in_dim(block_mask, position, 1, 1)[:, 0]

    def split_heads(matrix):
        return matrix.reshape(matrix.shape[0], HEADS, head_size)

    def pair_terms(query_block, grad_block, key_block, value_block, allowed):
        scores = (
            jnp.einsum(
                "qhe,khe->hqk",
                split_heads(query_block),
                split_heads(key_block),
                preferred_element_type=jnp.float32,
            )
            * temper
        )
        gates = jax.nn.sigmoid(scores)
        weights = (scores * gates * history_scale * allowed).astype(jnp.bfloat16)
        slopes = gates * (1.0 + scores * (1.0 - gates))
        attn_grad = jnp.einsum(
            "qhe,khe->hqk",
            split_heads(grad_block),
            split_heads(value_block),
            preferred_element_type=jnp.float32,
        )
        score_grad = (attn_grad * slopes * (history_scale * temper) * allowed).astype(jnp.bfloat16)
        return (weights, score_grad)

    zero_rows = jnp.zeros((tokens, features), jnp.float32)
    zero_terms = jnp.zeros((tokens * seq_count, features), jnp.float32)
    query_piece = lax.all_gather(queries, "seq", axis=0, tiled=True)
    grad_piece = lax.all_gather(cotangent, "seq", axis=0, tiled=True)
    block_rows = block_length(query_piece.shape[0])

    def advance(block_index, running):
        first_row = block_index * block_rows
        query_block = lax.dynamic_slice_in_dim(query_piece, first_row, block_rows, 0)
        grad_block = lax.dynamic_slice_in_dim(grad_piece, first_row, block_rows, 0)
        query_pos = first_row + jnp.arange(block_rows)
        query_blk = query_pos // tokens
        visible = jnp.any(
            (query_blk[:, None] == block_ids[None, :]) & (visible_col[None, :] == 1), axis=1
        ) | (query_blk == position)
        allowed = (visible[:, None] & (own_pos[None, :] <= query_pos[:, None])).astype(jnp.float32)

        def accumulate(current):
            weights, score_grad = pair_terms(query_block, grad_block, key_mat, value_mat, allowed)
            value_total = current[1] + jnp.einsum(
                "hqk,qhe->khe", weights, split_heads(grad_block), preferred_element_type=jnp.float32
            ).reshape(tokens, features)
            key_total = current[0] + jnp.einsum(
                "hqk,qhe->khe",
                score_grad,
                split_heads(query_block),
                preferred_element_type=jnp.float32,
            ).reshape(tokens, features)
            query_part = jnp.einsum(
                "hqk,khe->qhe", score_grad, split_heads(key_mat), preferred_element_type=jnp.float32
            ).reshape(block_rows, features)
            query_terms = lax.dynamic_update_slice(
                current[2], query_part, (first_row, jnp.int32(0))
            )
            return (key_total, value_total, query_terms)

        return lax.cond(jnp.any(allowed > 0), accumulate, lambda current: current, running)

    key_grad, value_grad, query_terms = lax.fori_loop(
        0, query_piece.shape[0] // block_rows, advance, (zero_rows, zero_rows, zero_terms)
    )
    query_grad = lax.psum_scatter(query_terms, "seq", scatter_dimension=0, tiled=True)
    stacked = jnp.concatenate([query_grad, key_grad, value_grad], axis=1).astype(jnp.bfloat16)
    input_grad = lax.dot_general(
        stacked, proj, (((1,), (1,)), ((), ())), preferred_element_type=jnp.float32
    ).astype(jnp.bfloat16)
    event_items = item_ids[0]
    owners = owner_of[event_items]
    slab_index = local_of[event_items]
    capacity = 2 * tokens // owner_count
    owner_hits = (owners[:, None] == jnp.arange(owner_count)[None, :]).astype(jnp.int32)
    slots = jnp.sum(jnp.cumsum(owner_hits, axis=0) * owner_hits, axis=1) - 1
    target = owners * capacity + slots
    send_rows = (
        jnp.zeros((owner_count * capacity, features), jnp.bfloat16)
        .at[target]
        .set(input_grad)
        .reshape(owner_count, capacity, features)
    )
    send_index = (
        jnp.full((owner_count * capacity,), -1, jnp.int32)
        .at[target]
        .set(slab_index)
        .reshape(owner_count, capacity)
    )
    got_rows, got_index = (
        lax.all_to_all(send_rows, "table", split_axis=0, concat_axis=0, tiled=True),
        lax.all_to_all(send_index, "table", split_axis=0, concat_axis=0, tiled=True),
    )
    slab_rows = table.shape[0]
    select = (got_index.reshape(-1)[None, :] == jnp.arange(slab_rows)[:, None]).astype(jnp.bfloat16)
    slab_grad = jnp.dot(select, got_rows.reshape(-1, features), preferred_element_type=jnp.float32)
    item_grad = lax.psum(slab_grad.astype(jnp.bfloat16), "seq").astype(jnp.float32)
    new_table, new_moment, new_second = adam_update(item_grad, moment, second, table)
    clamped = jnp.clip(got_index, 0, slab_rows - 1)
    replies = jnp.where(
        (got_index >= 0)[:, :, None], new_table[clamped], jnp.zeros((), jnp.bfloat16)
    )
    returned_rows = lax.all_to_all(replies, "table", split_axis=0, concat_axis=0, tiled=True)
    event_rows = returned_rows.reshape(owner_count * capacity, features)[target]
    return (new_table, new_moment, new_second, event_rows[None])


def solution(mesh):
    return jax.shard_map(
        body,
        mesh=mesh,
        in_specs=(
            P("table", "seq", None),
            P(),
            P("table", "seq", None),
            P(),
            P("table", "seq"),
            P(),
            P(),
            P("table", None),
            P("table", None),
            P("table"),
        ),
        out_specs=(P("table", None), P("table", None), P("table"), P("table", "seq", None)),
        check_vma=False,
    )
```

profile of v0, /device:TPU:1, one launch (start us, length us, event | category | flops | bytes accessed | tf_op | source)
XLA Modules:
  0.0 459.3 jit_solution(3907325187602014289)
XLA Ops:
  7.2 1.4 copy-done
  8.6 1.3 convolution_convert_fusion
  10.6 1.7 copy.42
  12.4 0.8 constant_dynamic-slice_fusion.2
  13.5 62.1 %all-gather.4.cloned.1.call-done = bf16[2048,512]{1,0:T(8,128)(2,1)} async-done(((bf16[128,512]{1,0:T(8,128)(2,1)}), bf16[2048,512]{1,0:T(8,128)(2,1)}) %all-gather.4.cloned.1.call-update) | async-done | bytes 2097168 | tf_op jit(solution)/shard_map/all_gather | solution.py:79
  75.5 4.0 copy.44
  79.5 61.6 %all-gather.6.cloned.1.call-done = bf16[1,2048,512]{1,2,0:T(8,128)(2,1)} async-done(((bf16[1,128,512]{1,2,0:T(8,128)(2,1)}), bf16[1,2048,512]{1,2,0:T(8,128)(2,1)}) %all-gather.6.cloned.1.call-update) | async-done | bytes 2097168 | tf_op jit(solution)/shard_map/all_gather | solution.py:80
  141.1 2.5 broadcast_in_dim.58
  143.6 27.1 %while.20 = (s32[]{:T(128)}, f32[128,512]{0,1:T(8,128)S(1)}, f32[128,512]{0,1:T(8,128)S(1)}, f32[2048,512]{0,1:T(8,128)}, s32[16,1]{0,1:T(1,128)S(1)}, /*index=5...) while((s32[]{:T(128)}, f32[128,512]{0,1:T(8,128)S(1)}, ...), condition=%wide.region_8.9_spmd.clone, body=%wide.region_3.8_spmd.clone.sunk | while | flops 691094656 | bytes 72766960 | solution.py:115
  143.8 1.0 and_convert_fusion.2
  145.4 11.8 %conditional.3 = ((f32[128,512]{0,1:T(8,128)S(1)}, f32[128,512]{0,1:T(8,128)S(1)}, f32[2048,512]{0,1:T(8,128)})) conditional(s32[]{:T(128)} %convert_element_type.86, (f32[128,512]{0,1:T(8,128)S(1)}, f32[128,512]{0,1:T(8,128)S(1)}, f32[2048,512]{0,1:T(8,128)}) %tuple.80, (s32[]{:T(128)}, bf16[2048,512]{0,1:T(8,128)(2,1)}, ...), branch_computations={%region_6.6_spmd, %region_7.7_spmd} | conditional | flops 690356224 | bytes 72220808 | solution.py:113
  145.4 1.3 constant_dynamic-slice_fusion.1
  146.7 1.3 constant_dynamic-slice_fusion
  148.0 0.8 fusion.32
  148.9 1.4 fusion.4
  150.3 2.4 multiply_convert_fusion.1
  153.3 0.8 fusion.33
  154.2 0.7 copy-done.1
  155.2 1.9 copy-done.2
  157.3 1.0 and_convert_fusion.2
  158.9 11.8 %conditional.3 = ((f32[128,512]{0,1:T(8,128)S(1)}, f32[128,512]{0,1:T(8,128)S(1)}, f32[2048,512]{0,1:T(8,128)})) conditional(s32[]{:T(128)} %convert_element_type.86, (f32[128,512]{0,1:T(8,128)S(1)}, f32[128,512]{0,1:T(8,128)S(1)}, f32[2048,512]{0,1:T(8,128)}) %tuple.80, (s32[]{:T(128)}, bf16[2048,512]{0,1:T(8,128)(2,1)}, ...), branch_computations={%region_6.6_spmd, %region_7.7_spmd} | conditional | flops 690356224 | bytes 72220808 | solution.py:113
  158.9 1.3 constant_dynamic-slice_fusion.1
  160.2 1.3 constant_dynamic-slice_fusion
  161.5 0.8 fusion.32
  162.4 1.4 fusion.4
  163.9 2.4 multiply_convert_fusion.1
  166.9 0.8 fusion.33
  167.7 0.7 copy-done.1
  168.7 1.9 copy-done.2
  171.5 1.1 gather_fusion
  173.0 1.1 gather_fusion.1
  174.3 1.0 scatter_custom_fusion
  175.3 0.7 all_to_all.12
  176.0 14.4 %all-to-all-start = ((s32[32,1,8]{2,1,0:T(1,128)}), s32[32,1,8]{2,1,0:T(1,128)S(1)}, u32[]{:S(2)}, u32[]{:S(2)}) async-start(s32[32,1,8]{2,1,0:T(1,128)} %bitcast.14), calls=%async_computation | async-start | bytes 32768 | tf_op jit(solution)/shard_map/all_to_all | solution.py:144
  190.4 72.2 %reduce-scatter.2.cloned.1.call-done = f32[128,512]{0,1:T(8,128)} async-done(((f32[2048,512]{0,1:T(8,128)}), f32[128,512]{0,1:T(8,128)}) %reduce-scatter.2.cloned.1.call-update) | async-done | bytes 262160 | tf_op jit(solution)/shard_map/reduce_scatter | solution.py:118
  262.6 1.0 convert.9
  264.2 1.7 scatter_custom_fusion.1
  265.9 14.8 %all-to-all-start.1 = ((bf16[32,8,512]{2,1,0:T(8,128)(2,1)}), bf16[32,8,512]{2,1,0:T(8,128)(2,1)S(1)}, u32[]{:S(2)}, u32[]{:S(2)}) async-start(bf16[32,8,512]{2,1,0:T(8,128)(2,1)} %bitcast.17), calls=%async_computation.2 | async-start | bytes 524288 | tf_op jit(solution)/shard_map/all_to_all | solution.py:143
  282.2 20.8 %all-to-all-done.1 = bf16[32,8,512]{2,1,0:T(8,128)(2,1)S(1)} async-done(((bf16[32,8,512]{2,1,0:T(8,128)(2,1)}), bf16[32,8,512]{2,1,0:T(8,128)(2,1)S(1)}, u32[]{:S(2)}, u32[]{:S(2)}) %all-to-all-start.1) | async-done | bytes 262176 | tf_op jit(solution)/shard_map/all_to_all | solution.py:143
  303.0 1.1 convolution_convert_fusion.1
  304.4 103.3 %all-reduce.2.cloned.1.call-done = bf16[512,512]{1,0:T(8,128)(2,1)} async-done(((bf16[512,512]{1,0:T(8,128)(2,1)}), bf16[512,512]{1,0:T(8,128)(2,1)}) %all-reduce.2.cloned.1.call-update) | async-done | bytes 524304 | tf_op jit(solution)/shard_map/psum | solution.py:149
  407.8 1.2 fusion.13
  409.6 2.5 subtract_convert_fusion
  412.1 1.2 gather_fusion.2
  413.2 0.8 bitcast_select_fusion
  414.0 15.0 %all-to-all-start.2 = ((bf16[32,8,512]{2,1,0:T(8,128)(2,1)}), bf16[32,8,512]{2,1,0:T(8,128)(2,1)S(1)}, u32[]{:S(2)}, u32[]{:S(2)}) async-start(bf16[32,8,512]{2,1,0:T(8,128)(2,1)} %bitcast_select_fusion), calls=%async_computation.3 | async-start | bytes 524288 | tf_op jit(solution)/shard_map/all_to_all | solution.py:155
  429.0 22.2 %all-to-all-done.2 = bf16[32,8,512]{2,1,0:T(8,128)(2,1)S(1)} async-done(((bf16[32,8,512]{2,1,0:T(8,128)(2,1)}), bf16[32,8,512]{2,1,0:T(8,128)(2,1)S(1)}, u32[]{:S(2)}, u32[]{:S(2)}) %all-to-all-start.2) | async-done | bytes 262176 | tf_op jit(solution)/shard_map/all_to_all | solution.py:155
  451.3 1.5 gather_fusion.3
  (71 shorter events, 7.7 us)
Async XLA Ops:
  7.2 1.4 copy-start
  7.2 68.4 %all-gather.4.cloned.1.call-start = ((), (), s32[]{:S(2)}) async-start(), calls=%async_computation.4 | async-start | bytes 2228224 | tf_op jit(solution)/shard_map/all_gather | solution.py:79
  10.6 130.5 %all-gather.6.cloned.1.call-start = ((), (), s32[]{:S(2)}) async-start(), calls=%async_computation.7 | async-start | bytes 2228224 | tf_op jit(solution)/shard_map/all_gather | solution.py:80
  12.3 250.2 %reduce-scatter.2.cloned.1.call-start = ((), (), s32[]{:S(2)}) async-start(), calls=%async_computation.5 | async-start | bytes 4456448 | tf_op jit(solution)/shard_map/reduce_scatter | solution.py:118
  152.7 2.2 copy-start.1
  155.2 2.0 copy-start.2
  166.2 2.2 copy-start.1
  168.7 2.0 copy-start.2
  170.7 0.7 copy-start.8
  170.7 0.9 copy-start.4
  170.7 2.3 copy-start.5
  171.3 237.6 %copy-start.7 = (f32[512]{0:T(512)S(1)}, f32[512]{0:T(512)}, u32[]{:S(2)}) copy-start(f32[512]{0:T(512)} %param.23) | copy-start | bytes 6148
  171.3 238.2 %copy-start.6 = (f32[512,512]{1,0:T(8,128)S(1)}, f32[512,512]{1,0:T(8,128)}, u32[]{:S(2)}) copy-start(f32[512,512]{1,0:T(8,128)} %param.22) | copy-start | bytes 3145732
  176.0 89.9 %all-to-all-start = ((s32[32,1,8]{2,1,0:T(1,128)}), s32[32,1,8]{2,1,0:T(1,128)S(1)}, u32[]{:S(2)}, u32[]{:S(2)}) async-start(s32[32,1,8]{2,1,0:T(1,128)} %bitcast.14), calls=%async_computation | async-start | bytes 32768 | tf_op jit(solution)/shard_map/all_to_all | solution.py:144
  265.9 37.1 %all-to-all-start.1 = ((bf16[32,8,512]{2,1,0:T(8,128)(2,1)}), bf16[32,8,512]{2,1,0:T(8,128)(2,1)S(1)}, u32[]{:S(2)}, u32[]{:S(2)}) async-start(bf16[32,8,512]{2,1,0:T(8,128)(2,1)} %bitcast.17), calls=%async_computation.2 | async-start | bytes 524288 | tf_op jit(solution)/shard_map/all_to_all | solution.py:143
  280.7 127.0 %all-reduce.2.cloned.1.call-start = ((), (), s32[]{:S(2)}) async-start(), calls=%async_computation.6 | async-start | bytes 1048576 | tf_op jit(solution)/shard_map/psum | solution.py:149
  412.1 40.7 %copy-start.3 = (bf16[512,512]{1,0:T(8,128)(2,1)}, bf16[512,512]{1,0:T(8,128)(2,1)S(1)}, u32[]{:S(2)}) copy-start(bf16[512,512]{1,0:T(8,128)(2,1)S(1)} %get-tuple-element.535) | copy-start | bytes 1572868
  414.0 37.2 %all-to-all-start.2 = ((bf16[32,8,512]{2,1,0:T(8,128)(2,1)}), bf16[32,8,512]{2,1,0:T(8,128)(2,1)S(1)}, u32[]{:S(2)}, u32[]{:S(2)}) async-start(bf16[32,8,512]{2,1,0:T(8,128)(2,1)} %bitcast_select_fusion), calls=%async_computation.3 | async-start | bytes 524288 | tf_op jit(solution)/shard_map/all_to_all | solution.py:155
Sparse Core Ops, SparseCore 0:
  11.6 63.9 all-gather.3
  79.1 61.9 all-gather.5
  170.8 91.6 reduce-scatter.1
  304.3 103.4 all-reduce.1
where the time goes:
time: 460 us; the launch traced here: 459 us
  waiting for transfers between devices  342 us (74%)
  starting transfers between devices  44.3 us (10%)
  local copies, waits for them, and re-layouts  32.5 us (7%)
  matrix products  14.9 us (3%)
  between operations  14 us (3%)
  other arithmetic  9.82 us (2%)
    psum x1, waiting for transfers between devices, body(): lax.psum(slab_grad.astype(jnp.bfloat16), 'seq').astype(jnp.float32)  103 us
    reduce_scatter x1, waiting for transfers between devices, body(): lax.psum_scatter(query_terms, 'seq', scatter_dimension=0, tiled=True)  72.2 us
    all_gather x1, waiting for transfers between devices, body(): query_piece = lax.all_gather(queries, 'seq', axis=0, tiled=True)  62.1 us
    all_gather x1, waiting for transfers between devices, body(): grad_piece = lax.all_gather(cotangent, 'seq', axis=0, tiled=True)  61.6 us
    all_to_all x1, waiting for transfers between devices, body(): lax.all_to_all(replies, 'table', split_axis=0, concat_axis=0, tiled=True)  22.2 us
    all_to_all x1, waiting for transfers between devices, body(): lax.all_to_all(send_rows, 'table', split_axis=0, concat_axis=0, tiled=True)  20.8 us
    all_to_all x1, starting transfers between devices, body(): lax.all_to_all(replies, 'table', split_axis=0, concat_axis=0, tiled=True)  15 us
    all_to_all x1, starting transfers between devices, body(): lax.all_to_all(send_rows, 'table', split_axis=0, concat_axis=0, tiled=True)  14.8 us
  transfers between devices with their start and end apart: 7, of which 6 were waited for; matrix products, arithmetic and copies ran while one was open for 3% of the time, Pallas kernels for 0%

commit v1 on v0

--- a/solution.py
+++ b/solution.py
@@ -146,7 +146,9 @@
     slab_rows = table.shape[0]
     select = (got_index.reshape(-1)[None, :] == jnp.arange(slab_rows)[:, None]).astype(jnp.bfloat16)
     slab_grad = jnp.dot(select, got_rows.reshape(-1, features), preferred_element_type=jnp.float32)
-    item_grad = lax.psum(slab_grad.astype(jnp.bfloat16), "seq").astype(jnp.float32)
+    item_grad = jnp.sum(lax.all_gather(slab_grad.astype(jnp.bfloat16), "seq"), axis=0).astype(
+        jnp.float32
+    )
     new_table, new_moment, new_second = adam_update(item_grad, moment, second, table)
     clamped = jnp.clip(got_index, 0, slab_rows - 1)
     replies = jnp.where(

time: 460 us -> 434 us (0.943)
  waiting for transfers between devices: 342 us -> 314 us
    psum x1 -> x0, waiting for transfers between devices: 103 us -> none  [body(): lax.psum(slab_grad.astype(jnp.bfloat16), 'seq').astype(jnp.float32)]
    all_gather x0 -> x1, waiting for transfers between devices: none -> 74.8 us  [body(): lax.all_gather(slab_grad.astype(jnp.bfloat16), 'seq')]
    reduce_sum x0 -> x1, other arithmetic: none -> 4.88 us  [body(): jnp.sum(lax.all_gather(slab_grad.astype(jnp.bfloat16), 'seq'), axis=0)]
  transfers between devices with their start and end apart: 7 -> 7, of which waited for: 6 -> 6; matrix products, arithmetic and copies ran while one was open for 3% -> 4% of each run, Pallas kernels for 0% -> 0%
where the time goes in v1:
time: 434 us; the launch traced here: 433 us
  waiting for transfers between devices  314 us (72%)
  starting transfers between devices  42.7 us (10%)
  local copies, waits for them, and re-layouts  32.5 us (7%)
  matrix products  14.9 us (3%)
  between operations  14 us (3%)
  other arithmetic  13.7 us (3%)
    all_gather x1, waiting for transfers between devices, body(): lax.all_gather(slab_grad.astype(jnp.bfloat16), 'seq')  74.8 us
    reduce_scatter x1, waiting for transfers between devices, body(): lax.psum_scatter(query_terms, 'seq', scatter_dimension=0, tiled=True)  72.2 us
    all_gather x1, waiting for transfers between devices, body(): query_piece = lax.all_gather(queries, 'seq', axis=0, tiled=True)  62.1 us
    all_gather x1, waiting for transfers between devices, body(): grad_piece = lax.all_gather(cotangent, 'seq', axis=0, tiled=True)  61.6 us
    all_to_all x1, waiting for transfers between devices, body(): lax.all_to_all(replies, 'table', split_axis=0, concat_axis=0, tiled=True)  22.2 us
    all_to_all x1, waiting for transfers between devices, body(): lax.all_to_all(send_rows, 'table', split_axis=0, concat_axis=0, tiled=True)  20.7 us
    all_to_all x1, starting transfers between devices, body(): lax.all_to_all(send_rows, 'table', split_axis=0, concat_axis=0, tiled=True)  14.8 us
    all_to_all x1, starting transfers between devices, body(): lax.all_to_all(send_index, 'table', split_axis=0, concat_axis=0, tiled=True)  14.4 us
  transfers between devices with their start and end apart: 7, of which 6 were waited for; matrix products, arithmetic and copies ran while one was open for 4% of the time, Pallas kernels for 0%

profile of v1, /device:TPU:1, one launch (start us, length us, event | category | flops | bytes accessed | tf_op | source)
XLA Modules:
  0.0 433.0 jit_solution(12166473410530913612)
XLA Ops:
  7.2 1.4 copy-done
  8.6 1.3 convolution_convert_fusion
  10.6 1.7 copy.42
  12.4 0.8 constant_dynamic-slice_fusion.2
  13.5 62.1 %all-gather.6.cloned.1.call-done = bf16[2048,512]{1,0:T(8,128)(2,1)} async-done(((bf16[128,512]{1,0:T(8,128)(2,1)}), bf16[2048,512]{1,0:T(8,128)(2,1)}) %all-gather.6.cloned.1.call-update) | async-done | bytes 2097168 | tf_op jit(solution)/shard_map/all_gather | solution.py:79
  75.5 4.0 copy.44
  79.5 61.6 %all-gather.8.cloned.1.call-done = bf16[1,2048,512]{1,2,0:T(8,128)(2,1)} async-done(((bf16[1,128,512]{1,2,0:T(8,128)(2,1)}), bf16[1,2048,512]{1,2,0:T(8,128)(2,1)}) %all-gather.8.cloned.1.call-update) | async-done | bytes 2097168 | tf_op jit(solution)/shard_map/all_gather | solution.py:80
  141.1 2.5 broadcast_in_dim.58
  143.6 27.1 %while.20 = (s32[]{:T(128)}, f32[128,512]{0,1:T(8,128)S(1)}, f32[128,512]{0,1:T(8,128)S(1)}, f32[2048,512]{0,1:T(8,128)}, s32[16,1]{0,1:T(1,128)S(1)}, /*index=5...) while((s32[]{:T(128)}, f32[128,512]{0,1:T(8,128)S(1)}, ...), condition=%wide.region_8.9_spmd.clone, body=%wide.region_3.8_spmd.clone.sunk | while | flops 691094656 | bytes 72766960 | solution.py:115
  143.8 1.0 and_convert_fusion.2
  145.4 11.8 %conditional.3 = ((f32[128,512]{0,1:T(8,128)S(1)}, f32[128,512]{0,1:T(8,128)S(1)}, f32[2048,512]{0,1:T(8,128)})) conditional(s32[]{:T(128)} %convert_element_type.88, (f32[128,512]{0,1:T(8,128)S(1)}, f32[128,512]{0,1:T(8,128)S(1)}, f32[2048,512]{0,1:T(8,128)}) %tuple.80, (s32[]{:T(128)}, bf16[2048,512]{0,1:T(8,128)(2,1)}, ...), branch_computations={%region_6.6_spmd, %region_7.7_spmd} | conditional | flops 690356224 | bytes 72220808 | solution.py:113
  145.4 1.3 constant_dynamic-slice_fusion.1
  146.7 1.3 constant_dynamic-slice_fusion
  148.0 0.8 fusion.32
  148.9 1.4 fusion.4
  150.3 2.4 multiply_convert_fusion.1
  153.3 0.8 fusion.33
  154.2 0.7 copy-done.1
  155.2 1.9 copy-done.2
  157.3 1.0 and_convert_fusion.2
  158.9 11.8 %conditional.3 = ((f32[128,512]{0,1:T(8,128)S(1)}, f32[128,512]{0,1:T(8,128)S(1)}, f32[2048,512]{0,1:T(8,128)})) conditional(s32[]{:T(128)} %convert_element_type.88, (f32[128,512]{0,1:T(8,128)S(1)}, f32[128,512]{0,1:T(8,128)S(1)}, f32[2048,512]{0,1:T(8,128)}) %tuple.80, (s32[]{:T(128)}, bf16[2048,512]{0,1:T(8,128)(2,1)}, ...), branch_computations={%region_6.6_spmd, %region_7.7_spmd} | conditional | flops 690356224 | bytes 72220808 | solution.py:113
  158.9 1.3 constant_dynamic-slice_fusion.1
  160.2 1.3 constant_dynamic-slice_fusion
  161.5 0.8 fusion.32
  162.5 1.4 fusion.4
  163.9 2.4 multiply_convert_fusion.1
  166.9 0.8 fusion.33
  167.7 0.7 copy-done.1
  168.7 1.9 copy-done.2
  171.5 1.1 gather_fusion
  173.0 1.1 gather_fusion.1
  174.3 1.0 scatter_custom_fusion
  175.3 0.7 all_to_all.12
  176.0 14.4 %all-to-all-start = ((s32[32,1,8]{2,1,0:T(1,128)}), s32[32,1,8]{2,1,0:T(1,128)S(1)}, u32[]{:S(2)}, u32[]{:S(2)}) async-start(s32[32,1,8]{2,1,0:T(1,128)} %bitcast.14), calls=%async_computation | async-start | bytes 32768 | tf_op jit(solution)/shard_map/all_to_all | solution.py:144
  190.4 72.2 %reduce-scatter.2.cloned.1.call-done = f32[128,512]{0,1:T(8,128)} async-done(((f32[2048,512]{0,1:T(8,128)}), f32[128,512]{0,1:T(8,128)}) %reduce-scatter.2.cloned.1.call-update) | async-done | bytes 262160 | tf_op jit(solution)/shard_map/reduce_scatter | solution.py:118
  262.6 1.0 convert.10
  264.2 1.7 scatter_custom_fusion.1
  266.0 14.8 %all-to-all-start.1 = ((bf16[32,8,512]{2,1,0:T(8,128)(2,1)}), bf16[32,8,512]{2,1,0:T(8,128)(2,1)S(1)}, u32[]{:S(2)}, u32[]{:S(2)}) async-start(bf16[32,8,512]{2,1,0:T(8,128)(2,1)} %bitcast.17), calls=%async_computation.2 | async-start | bytes 524288 | tf_op jit(solution)/shard_map/all_to_all | solution.py:143
  282.3 20.7 %all-to-all-done.1 = bf16[32,8,512]{2,1,0:T(8,128)(2,1)S(1)} async-done(((bf16[32,8,512]{2,1,0:T(8,128)(2,1)}), bf16[32,8,512]{2,1,0:T(8,128)(2,1)S(1)}, u32[]{:S(2)}, u32[]{:S(2)}) %all-to-all-start.1) | async-done | bytes 262176 | tf_op jit(solution)/shard_map/all_to_all | solution.py:143
  303.1 1.1 convolution_convert_fusion.1
  304.6 74.8 %all-gather.10.cloned.1.call-done = bf16[8192,512]{1,0:T(8,128)(2,1)} async-done(((bf16[512,512]{1,0:T(8,128)(2,1)}), bf16[8192,512]{1,0:T(8,128)(2,1)}) %all-gather.10.cloned.1.call-update) | async-done | bytes 8388624 | tf_op jit(solution)/shard_map/all_gather | solution.py:149
  379.4 4.9 %reduce_sum.31 = bf16[512,512]{1,0:T(8,128)(2,1)S(1)} reduce(bf16[16,512,512]{2,1,0:T(8,128)(2,1)} %bitcast.66, bf16[]{:T(256)} %constant.177.clone.1), dimensions={0}, to_apply=%region_11.12 | reduce | flops 3932160 | bytes 8912898 | tf_op jit(solution)/shard_map/reduce_sum | solution.py:149
  385.0 2.5 subtract_convert_fusion
  387.6 1.2 gather_fusion.2
  388.7 0.8 bitcast_select_fusion
  389.5 13.2 %all-to-all-start.2 = ((bf16[32,8,512]{2,1,0:T(8,128)(2,1)}), bf16[32,8,512]{2,1,0:T(8,128)(2,1)S(1)}, u32[]{:S(2)}, u32[]{:S(2)}) async-start(bf16[32,8,512]{2,1,0:T(8,128)(2,1)} %bitcast_select_fusion), calls=%async_computation.3 | async-start | bytes 524288 | tf_op jit(solution)/shard_map/all_to_all | solution.py:157
  402.7 22.2 %all-to-all-done.2 = bf16[32,8,512]{2,1,0:T(8,128)(2,1)S(1)} async-done(((bf16[32,8,512]{2,1,0:T(8,128)(2,1)}), bf16[32,8,512]{2,1,0:T(8,128)(2,1)S(1)}, u32[]{:S(2)}, u32[]{:S(2)}) %all-to-all-start.2) | async-done | bytes 262176 | tf_op jit(solution)/shard_map/all_to_all | solution.py:157
  425.0 1.5 gather_fusion.3
  (72 shorter events, 8.0 us)
Async XLA Ops:
  7.2 1.4 copy-start
  7.2 68.4 %all-gather.6.cloned.1.call-start = ((), (), s32[]{:S(2)}) async-start(), calls=%async_computation.4 | async-start | bytes 2228224 | tf_op jit(solution)/shard_map/all_gather | solution.py:79
  10.6 130.5 %all-gather.8.cloned.1.call-start = ((), (), s32[]{:S(2)}) async-start(), calls=%async_computation.6 | async-start | bytes 2228224 | tf_op jit(solution)/shard_map/all_gather | solution.py:80
  12.3 250.3 %reduce-scatter.2.cloned.1.call-start = ((), (), s32[]{:S(2)}) async-start(), calls=%async_computation.5 | async-start | bytes 4456448 | tf_op jit(solution)/shard_map/reduce_scatter | solution.py:118
  152.7 2.2 copy-start.1
  155.2 2.0 copy-start.2
  166.2 2.2 copy-start.1
  168.7 2.0 copy-start.2
  170.7 0.7 copy-start.8
  170.7 0.9 copy-start.4
  170.7 2.3 copy-start.5
  176.0 90.0 %all-to-all-start = ((s32[32,1,8]{2,1,0:T(1,128)}), s32[32,1,8]{2,1,0:T(1,128)S(1)}, u32[]{:S(2)}, u32[]{:S(2)}) async-start(s32[32,1,8]{2,1,0:T(1,128)} %bitcast.14), calls=%async_computation | async-start | bytes 32768 | tf_op jit(solution)/shard_map/all_to_all | solution.py:144
  266.0 37.1 %all-to-all-start.1 = ((bf16[32,8,512]{2,1,0:T(8,128)(2,1)}), bf16[32,8,512]{2,1,0:T(8,128)(2,1)S(1)}, u32[]{:S(2)}, u32[]{:S(2)}) async-start(bf16[32,8,512]{2,1,0:T(8,128)(2,1)} %bitcast.17), calls=%async_computation.2 | async-start | bytes 524288 | tf_op jit(solution)/shard_map/all_to_all | solution.py:143
  280.8 98.6 %all-gather.10.cloned.1.call-start = ((), (), s32[]{:S(2)}) async-start(), calls=%async_computation.7 | async-start | bytes 8912896 | tf_op jit(solution)/shard_map/all_gather | solution.py:149
  379.4 5.1 %copy-start.7 = (f32[512]{0:T(512)S(1)}, f32[512]{0:T(512)}, u32[]{:S(2)}) copy-start(f32[512]{0:T(512)} %param.23) | copy-start | bytes 6148
  379.4 5.7 %copy-start.6 = (bf16[512,512]{1,0:T(8,128)(2,1)S(1)}, bf16[512,512]{1,0:T(8,128)(2,1)}, u32[]{:S(2)}) copy-start(bf16[512,512]{1,0:T(8,128)(2,1)} %param.21) | copy-start | bytes 1572868
  387.6 38.9 %copy-start.3 = (bf16[512,512]{1,0:T(8,128)(2,1)}, bf16[512,512]{1,0:T(8,128)(2,1)S(1)}, u32[]{:S(2)}) copy-start(bf16[512,512]{1,0:T(8,128)(2,1)S(1)} %get-tuple-element.535) | copy-start | bytes 1572868
  389.5 35.4 %all-to-all-start.2 = ((bf16[32,8,512]{2,1,0:T(8,128)(2,1)}), bf16[32,8,512]{2,1,0:T(8,128)(2,1)S(1)}, u32[]{:S(2)}, u32[]{:S(2)}) async-start(bf16[32,8,512]{2,1,0:T(8,128)(2,1)} %bitcast_select_fusion), calls=%async_computation.3 | async-start | bytes 524288 | tf_op jit(solution)/shard_map/all_to_all | solution.py:157
Sparse Core Ops, SparseCore 0:
  11.6 63.9 all-gather.5
  79.1 61.9 all-gather.7
  170.8 91.7 reduce-scatter.1
  304.3 75.0 all-gather.9
